TPU v7x, 768 devices: a whole 4x8x12 slice. The times are simulated.
768 devices in a mesh: face: 16 (over y, core), blk: 48 (over z, x).
Axes of the slice: x: 4, y: 8, z: 12, core: 2. Of those that a mesh axis runs over, the one named last changes fastest.
Arguments:
- isotope_ratios: float32 [3, 32, 256, 6144], P(None, None, 'face', 'blk'), may hold values from 2 to 4
- advecting_velocity: float32 [2, 32, 256, 6144], P(None, None, 'face', 'blk'), may hold values from -1 to 1
- metric_scaling: float32 [256, 6144], P('face', 'blk'), may hold values from 0.5 to 2
- thermal_state: float32 [16, 32, 55296], P('face', None, 'blk'), may hold values from 255 to 300
- outgoing_site_order: int32 [16, 55296], P('face', 'blk'), may hold values from 0 to 1151, as said below
- daytime_indicator: int32 [16, 55296], P('face', 'blk'), may hold values from 0 to 1, as said below
Outputs:
- new_tracers: float32 [3, 32, 256, 6144], P(None, None, 'face', 'blk')
- phys_tracers: float32 [16, 3, 32, 55296], P('face', None, None, 'blk')
Inputs may be any that keep to these rules, and one draw needn't show every extreme that they name: `outgoing_site_order`: the 1152 entries that belong to one device are a permutation of 0 .. 1151; the device's entries k of its block name the local column it sends in position k, to blk peer k // 24. `daytime_indicator`: each device sends the same number of day columns to every peer along blk, and every physics batch (the 1152 columns one device receives) holds exactly 576 day columns.
All inputs are finite; a program needn't handle non-finite values.
Results may differ from a plain program's by a relative error of at most 0.0003.
Values sent between devices are 32-bit elements; how exact they have to be, the bound alone decides.
A program may use at most 32 MiB of HBM per device.

v0:
```python
import math

import jax
import jax.numpy as jnp
import numpy as np
from jax import lax
from jax.sharding import PartitionSpec as P

time_step = 0.006
absorb_coef = 0.02
heat_gain = 100.0
sat_base = 3.0
clausius = 0.07
ref_temp = 280.0


def extended(x, sides, width):
    for axis, dim in sides:
        devices, length = (lax.axis_size(axis), x.shape[dim])
        up = [(i, (i + 1) % devices) for i in range(devices)]
        down = [(j, i) for i, j in up]
        last = lax.slice_in_dim(x, length - width, length, axis=dim)
        initial = lax.slice_in_dim(x, 0, width, axis=dim)
        before = lax.ppermute(last, axis, up)
        after = lax.ppermute(initial, axis, down)
        x = jnp.concatenate([before, x, after], axis=dim)
    return x


def gll_tables():
    inv_root = 1.0 / math.sqrt(5.0)
    gll_nodes = np.array([-1.0, -inv_root, inv_root, 1.0])
    legendre = (5.0 * gll_nodes**3 - 3.0 * gll_nodes) / 2.0
    deriv_matrix = np.zeros((4, 4))
    for row_index in range(4):
        for col_index in range(4):
            if row_index != col_index:
                deriv_matrix[row_index, col_index] = legendre[row_index] / (
                    legendre[col_index] * (gll_nodes[row_index] - gll_nodes[col_index])
                )
    deriv_matrix[0, 0] = -3.0
    deriv_matrix[3, 3] = 3.0
    weights = np.array([1.0, 5.0, 5.0, 1.0]) / 6.0
    return (deriv_matrix, weights)


def add_partners(padded, axis_dim):
    span_len = padded.shape[axis_dim] - 2
    centre = lax.slice_in_dim(padded, 1, span_len + 1, axis=axis_dim)
    following = lax.slice_in_dim(padded, 2, span_len + 2, axis=axis_dim)
    before = lax.slice_in_dim(padded, 0, span_len, axis=axis_dim)
    bcast_shape = [1] * padded.ndim
    bcast_shape[axis_dim] = span_len
    position = (jnp.arange(span_len) % 4).reshape(bcast_shape)
    return centre + jnp.where(position == 3, following, 0.0) + jnp.where(position == 0, before, 0.0)


def radiative_warming(vapour):
    depth = jnp.cumsum(absorb_coef * vapour, axis=0)
    return heat_gain * absorb_coef * vapour * jnp.exp(-depth)


def condense(vapour, heavy, deuter, warmed_profiles):
    saturation = sat_base * jnp.exp(clausius * (warmed_profiles - ref_temp))
    remain = jnp.minimum(vapour, saturation)
    log_ratio = jnp.log(remain / vapour)
    inverse = 1.0 / warmed_profiles
    alpha_heavy = jnp.exp(1137.0 * inverse * inverse - 0.4156 * inverse - 0.0020667)
    alpha_deut = jnp.exp(24844.0 * inverse * inverse - 76.248 * inverse + 0.052612)
    return jnp.stack(
        [remain, heavy * jnp.exp(alpha_heavy * log_ratio), deuter * jnp.exp(alpha_deut * log_ratio)]
    )


def on_device(
    isotope_ratios,
    advecting_velocity,
    metric_scaling,
    thermal_state,
    outgoing_site_order,
    daytime_indicator,
):
    deriv_np, weight_np = gll_tables()
    size_x, size_y = metric_scaling.shape
    layer_total = isotope_ratios.shape[1]
    sites_per_processor = outgoing_site_order.shape[1]
    block_width = math.gcd(size_y, 128)
    kron_first = jnp.asarray(np.kron(np.eye(size_x // 4), deriv_np), jnp.float32)
    kron_second = jnp.asarray(np.kron(np.eye(block_width // 4), deriv_np), jnp.float32)
    outer_weight = np.outer(np.tile(weight_np, size_x // 4), np.tile(weight_np, size_y // 4))
    node_mass = jnp.asarray(outer_weight, jnp.float32) * metric_scaling
    flux_x = metric_scaling * advecting_velocity[0] * isotope_ratios
    flux_y = metric_scaling * advecting_velocity[1] * isotope_ratios
    grad_x = jnp.einsum("ij,sljy->sliy", kron_first, flux_x, precision=lax.Precision.HIGHEST)
    shaped_y = flux_y.reshape(3, layer_total, size_x, size_y // block_width, block_width)
    grad_y = jnp.einsum("slxab,cb->slxac", shaped_y, kron_second, precision=lax.Precision.HIGHEST)
    tendency = -(grad_x + grad_y.reshape(3, layer_total, size_x, size_y)) / metric_scaling
    payload = jnp.concatenate(
        [(node_mass * tendency).reshape(3 * layer_total, size_x, size_y), node_mass[None]], axis=0
    )
    padded = extended(payload, (("face", 1), ("blk", 2)), 1)
    summed = add_partners(add_partners(padded, 1), 2)
    ratio = summed[: 3 * layer_total] / summed[3 * layer_total]
    new_tracers = isotope_ratios + time_step * ratio.reshape(3, layer_total, size_x, size_y)
    shaped = new_tracers.reshape(3, layer_total, size_x // 4, 4, size_y // 4, 4)[:, :, :, :3, :, :3]
    profile_list = shaped.reshape(3, layer_total, sites_per_processor)
    send_perm = outgoing_site_order[0]
    profile_warmth = thermal_state[0]
    state = jnp.concatenate(
        [profile_list.reshape(3 * layer_total, sites_per_processor), profile_warmth], axis=0
    )
    moved_state, moved_mask = (
        lax.all_to_all(state[:, send_perm], "blk", split_axis=1, concat_axis=1, tiled=True),
        lax.all_to_all(
            daytime_indicator[:, send_perm], "blk", split_axis=1, concat_axis=1, tiled=True
        ),
    )
    vapour = moved_state[0:layer_total]
    heavy = moved_state[layer_total : 2 * layer_total]
    deuter = moved_state[2 * layer_total : 3 * layer_total]
    moved_temps = moved_state[3 * layer_total :]
    warmed_profiles = moved_temps + jnp.where(
        moved_mask[0][None, :] == 1, radiative_warming(vapour), 0.0
    )
    result = condense(vapour, heavy, deuter, warmed_profiles)
    return (new_tracers, result[None])


def solution(mesh):
    placed = (
        P(None, None, "face", "blk"),
        P(None, None, "face", "blk"),
        P("face", "blk"),
        P("face", None, "blk"),
        P("face", "blk"),
        P("face", "blk"),
    )
    return jax.shard_map(
        on_device,
        mesh=mesh,
        in_specs=placed,
        out_specs=(P(None, None, "face", "blk"), P("face", None, None, "blk")),
        check_vma=False,
    )
```

profile of v0, /device:TPU:24, one launch (start us, length us, event | category | flops | bytes accessed | tf_op | source)
XLA Modules:
  0.0 101.4 jit_solution(10490264477427895018)
XLA Ops:
  0.7 1.1 %multiply_bitcast_fusion = (f32[32,16,128]{2,1,0:T(8,128)S(1)}, f32[32,16,128]{2,1,0:T(8,128)S(1)}) fusion(f32[2,32,16,128]{3,2,1,0:T(8,128)} %param.10, f32[16,128]{1,0:T(8,128)} %param.11), kind=kLoop, calls=%fused_computation.25 | loop fusion | flops 131072 | bytes 1056768 | tf_op jit(solution)/shard_map/mul | solution.py:93
  1.8 0.7 mul.222
  2.6 1.5 %convolution_bitcast_fusion = f32[3,32,16,128]{3,2,1,0:T(8,128)S(1)} fusion(f32[16,16,1,1]{1,0,3,2:T(8,128)} %constant.82, f32[3,32,16,128]{3,2,1,0:T(8,128)S(1)} %copy-done.1, f32[32,16,128]{2,1,0:T(8,128)S(1)} %get-tuple-element.15), kind=kOutput, calls=%fused_computation.9 | convolution fusion | flops 37945344 | bytes 1836032 | tf_op jit(solution)/shard_map/ij,sljy->sliy/dot_general | solution.py:94
  4.1 0.8 fusion.4
  5.0 1.7 %collective-permute-start.1 = (f32[97,1,128]{2,1,0:T(1,128)S(1)}, f32[97,1,128]{2,1,0:T(1,128)S(1)}, u32[]{:S(2)}, u32[]{:S(2)}) collective-permute-start(f32[97,1,128]{2,1,0:T(1,128)S(1)} %get-tuple-element.9), channel_id=1, source_target_pairs={{48,0},{96,48},{144,96},{192,144},{240,192},{288,240},{336,288},{3... | collective-permute-start | bytes 149000 | tf_op jit(solution)/shard_map/ppermute | solution.py:25
  6.8 6.5 %gather_fusion.1 = s32[1152]{0:T(1024)S(1)} fusion(s32[1152]{0:T(1024)S(1)} %reduce.1, s32[2048]{0:T(1024)S(1)} %pad_clamp_fusion), kind=kCustom, calls=%fused_computation.1 | custom fusion | bytes 13824 | tf_op jit(solution)/shard_map/gather | solution.py:115
  13.3 0.7 all_to_all.14
  14.0 18.5 %all-to-all-start.1 = ((s32[1,48,24]{2,0,1:T(1,128)}), s32[1,48,24]{2,0,1:T(1,128)}, u32[]{:S(2)}, u32[]{:S(2)}) async-start(s32[1,48,24]{2,0,1:T(1,128)} %bitcast.17), calls=%async_computation.1 | async-start | bytes 49152 | tf_op jit(solution)/shard_map/all_to_all | solution.py:114
  32.5 0.6 broadcast_compare_fusion.2
  34.0 3.5 %collective-permute-start.2 = (f32[97,18,1]{0,2,1:T(1,128)S(1)}, f32[97,18,1]{0,2,1:T(1,128)S(1)}, u32[]{:S(2)}, u32[]{:S(2)}) collective-permute-start(f32[97,18,1]{0,2,1:T(1,128)S(1)} %copy.36), channel_id=1, source_target_pairs={{0,1},{1,2},{2,3},{3,4},{4,5},{5,6},{6,7},{7,8},{8,9},{9,10},{10,1... | collective-permute-start | bytes 20960 | tf_op jit(solution)/shard_map/ppermute | solution.py:24
  37.9 5.7 %collective-permute-start.3 = (f32[97,18,1]{0,2,1:T(1,128)S(1)}, f32[97,18,1]{0,2,1:T(1,128)S(1)}, u32[]{:S(2)}, u32[]{:S(2)}) collective-permute-start(f32[97,18,1]{0,2,1:T(1,128)S(1)} %copy.37), channel_id=1, source_target_pairs={{1,0},{2,1},{3,2},{4,3},{5,4},{6,5},{7,6},{8,7},{9,8},{10,9},{11,1... | collective-permute-start | bytes 20960 | tf_op jit(solution)/shard_map/ppermute | solution.py:25
  43.6 1.1 %copy.42 = f32[1,32,1152]{1,2,0:T(8,128)} copy(f32[1,32,1152]{2,1,0:T(8,128)S(1)} %copy-done.4) | data formatting | bytes 294912 | tf_op args[3]
  45.8 1.5 %pad_maximum_fusion = f32[97,18,130]{2,1,0:T(8,128)S(1)} fusion(f32[97,18,1]{2,1,0:T(8,128)S(1)} %copy.39, f32[97,1,128]{2,1,0:T(1,128)S(1)} %collective-permute-done.1, f32[1,16,128]{2,1,0:T(8,128)S(1)} %bitcast.54, f32[96,16,128]{2,1,0:T(8,128)S(1)} %bitcast.45, f32[97,1,128]{2,1,0:T(1,128)S(1)} %collective-permute-done, f32[97,18,1]{2,1,0:T(8,128)S(1)} %copy.38), kind=kLoop, calls=%fused_computation.2 | loop fusion | flops 1134900 | bytes 1815840 | tf_op jit(solution)/shard_map/concatenate | solution.py:26
  48.3 1.0 %copy-done.2 = f32[3,32,16,128]{3,2,1,0:T(8,128)S(1)} copy-done((f32[3,32,16,128]{3,2,1,0:T(8,128)S(1)}, f32[3,32,16,128]{3,2,1,0:T(8,128)}, u32[]{:S(2)}) %copy-start.2) | copy-done | bytes 786456
  49.4 1.0 add.109
  50.3 2.0 %copy.40 = f32[3,32,16,128]{1,3,2,0:T(8,128)S(1)} copy(f32[3,32,16,128]{3,2,1,0:T(8,128)} %add.109) | data formatting | bytes 1572864 | tf_op jit(solution)/shard_map/add | solution.py:104
  52.6 1.2 %copy.41 = f32[3,32,4,3,32,3]{1,0,5,4,3,2:T(4,128)S(1)} copy(f32[3,32,4,3,32,3]{1,5,4,3,2,0:T(4,128)S(1)} %slice.106) | data formatting | bytes 884736 | tf_op jit(solution)/shard_map/slice | solution.py:105
  53.8 0.9 reshape_reshape.3
  55.1 3.1 %gather_fusion = f32[1152,128]{1,0:T(8,128)} fusion(f32[128,1152]{0,1:T(8,128)S(1)} %pad_maximum_fusion.2, s32[2048]{0:T(1024)S(1)} %pad_clamp_fusion), kind=kCustom, calls=%fused_computation | custom fusion | bytes 1184256 | tf_op jit(solution)/shard_map/gather | solution.py:113
  58.2 12.4 %all-to-all-start = ((f32[128,48,24]{0,2,1:T(8,128)}), f32[128,48,24]{0,2,1:T(8,128)S(1)}, u32[]{:S(2)}, u32[]{:S(2)}) async-start(f32[128,48,24]{0,2,1:T(8,128)} %bitcast.15), calls=%async_computation | async-start | bytes 1179648 | tf_op jit(solution)/shard_map/all_to_all | solution.py:113
  70.6 0.8 compare_reduce_fusion
  71.5 26.3 %all-to-all-done = f32[128,48,24]{0,2,1:T(8,128)S(1)} async-done(((f32[128,48,24]{0,2,1:T(8,128)}), f32[128,48,24]{0,2,1:T(8,128)S(1)}, u32[]{:S(2)}, u32[]{:S(2)}) %all-to-all-start) | async-done | bytes 589856 | tf_op jit(solution)/shard_map/all_to_all | solution.py:113
  97.8 0.5 fusion.29
  100.6 0.8 maximum_bitcast_fusion
  (54 shorter events, 6.5 us)
Async XLA Ops:
  0.6 6.2 %copy-start = (s32[1,1152]{1,0:T(1,128)S(1)}, s32[1,1152]{1,0:T(1,128)}, u32[]{:S(2)}) copy-start(s32[1,1152]{1,0:T(1,128)} %param.14) | copy-start | bytes 13828
  0.6 3.4 %copy-start.9 = (f32[128,128,1,1]{1,0,3,2:T(8,128)S(1)}, f32[128,128,1,1]{1,0,3,2:T(8,128)}, u32[]{:S(2)}) copy-start(f32[128,128,1,1]{1,0,3,2:T(8,128)} %constant.83) | copy-start | bytes 196612
  0.7 3.4 %copy-start.5 = (f32[16,128]{1,0:T(8,128)S(1)}, f32[16,128]{1,0:T(8,128)}, u32[]{:S(2)}) copy-start(f32[16,128]{1,0:T(8,128)} %param.11) | copy-start | bytes 24580
  0.7 1.9 %copy-start.1 = (f32[3,32,16,128]{3,2,1,0:T(8,128)S(1)}, f32[3,32,16,128]{3,2,1,0:T(8,128)}, u32[]{:S(2)}) copy-start(f32[3,32,16,128]{3,2,1,0:T(8,128)} %param.9) | copy-start | bytes 2359300
  4.1 2.7 %copy-start.6 = (s32[1,1152]{1,0:T(1,128)S(1)}, s32[1,1152]{1,0:T(1,128)}, u32[]{:S(2)}) copy-start(s32[1,1152]{1,0:T(1,128)} %param.13) | copy-start | bytes 13828
  5.0 28.1 %collective-permute-start = (f32[97,1,128]{2,1,0:T(1,128)S(1)}, f32[97,1,128]{2,1,0:T(1,128)S(1)}, u32[]{:S(2)}, u32[]{:S(2)}) collective-permute-start(f32[97,1,128]{2,1,0:T(1,128)S(1)} %get-tuple-element.8), channel_id=1, source_target_pairs={{0,48},{48,96},{96,144},{144,192},{192,240},{240,288},{288,336},{3... | collective-permute-start | bytes 149000 | tf_op jit(solution)/shard_map/ppermute | solution.py:24
  5.0 28.1 %collective-permute-start.1 = (f32[97,1,128]{2,1,0:T(1,128)S(1)}, f32[97,1,128]{2,1,0:T(1,128)S(1)}, u32[]{:S(2)}, u32[]{:S(2)}) collective-permute-start(f32[97,1,128]{2,1,0:T(1,128)S(1)} %get-tuple-element.9), channel_id=1, source_target_pairs={{48,0},{96,48},{144,96},{192,144},{240,192},{288,240},{336,288},{3... | collective-permute-start | bytes 149000 | tf_op jit(solution)/shard_map/ppermute | solution.py:25
  14.0 44.2 %all-to-all-start.1 = ((s32[1,48,24]{2,0,1:T(1,128)}), s32[1,48,24]{2,0,1:T(1,128)}, u32[]{:S(2)}, u32[]{:S(2)}) async-start(s32[1,48,24]{2,0,1:T(1,128)} %bitcast.17), calls=%async_computation.1 | async-start | bytes 49152 | tf_op jit(solution)/shard_map/all_to_all | solution.py:114
  33.7 10.0 %copy-start.4 = (f32[1,32,1152]{2,1,0:T(8,128)S(1)}, f32[1,32,1152]{2,1,0:T(8,128)}, u32[]{:S(2)}) copy-start(f32[1,32,1152]{2,1,0:T(8,128)} %param.12) | copy-start | bytes 442372
  34.0 10.7 %collective-permute-start.2 = (f32[97,18,1]{0,2,1:T(1,128)S(1)}, f32[97,18,1]{0,2,1:T(1,128)S(1)}, u32[]{:S(2)}, u32[]{:S(2)}) collective-permute-start(f32[97,18,1]{0,2,1:T(1,128)S(1)} %copy.36), channel_id=1, source_target_pairs={{0,1},{1,2},{2,3},{3,4},{4,5},{5,6},{6,7},{7,8},{8,9},{9,10},{10,1... | collective-permute-start | bytes 20960 | tf_op jit(solution)/shard_map/ppermute | solution.py:24
  37.9 7.3 %collective-permute-start.3 = (f32[97,18,1]{0,2,1:T(1,128)S(1)}, f32[97,18,1]{0,2,1:T(1,128)S(1)}, u32[]{:S(2)}, u32[]{:S(2)}) collective-permute-start(f32[97,18,1]{0,2,1:T(1,128)S(1)} %copy.37), channel_id=1, source_target_pairs={{1,0},{2,1},{3,2},{4,3},{5,4},{6,5},{7,6},{8,7},{9,8},{10,9},{11,1... | collective-permute-start | bytes 20960 | tf_op jit(solution)/shard_map/ppermute | solution.py:25
  45.7 1.5 %copy-start.7 = (pred[16]{0:T(512)(128)(4,1)S(1)}, pred[16]{0:T(512)(128)(4,1)}, u32[]{:S(2)}) copy-start(pred[16]{0:T(512)(128)(4,1)} %get-tuple-element.18) | copy-start | bytes 52
  45.8 1.5 %copy-start.8 = (pred[16]{0:T(512)(128)(4,1)S(1)}, pred[16]{0:T(512)(128)(4,1)}, u32[]{:S(2)}) copy-start(pred[16]{0:T(512)(128)(4,1)} %get-tuple-element.19) | copy-start | bytes 52
  48.2 1.1 %copy-start.2 = (f32[3,32,16,128]{3,2,1,0:T(8,128)S(1)}, f32[3,32,16,128]{3,2,1,0:T(8,128)}, u32[]{:S(2)}) copy-start(f32[3,32,16,128]{3,2,1,0:T(8,128)} %param.9) | copy-start | bytes 2359300
  53.8 1.1 %copy-start.3 = (f32[1,32,1152]{1,2,0:T(8,128)S(1)}, f32[1,32,1152]{1,2,0:T(8,128)}, u32[]{:S(2)}) copy-start(f32[1,32,1152]{1,2,0:T(8,128)} %copy.42) | copy-start | bytes 442372
  58.2 39.6 %all-to-all-start = ((f32[128,48,24]{0,2,1:T(8,128)}), f32[128,48,24]{0,2,1:T(8,128)S(1)}, u32[]{:S(2)}, u32[]{:S(2)}) async-start(f32[128,48,24]{0,2,1:T(8,128)} %bitcast.15), calls=%async_computation | async-start | bytes 1179648 | tf_op jit(solution)/shard_map/all_to_all | solution.py:113
where the time goes:
time: 102 us; the launch traced here: 101 us
  starting transfers between devices  41.8 us (41%)
  waiting for transfers between devices  26.3 us (26%)
  local copies, waits for them, and re-layouts  21.4 us (21%)
  other arithmetic  8.54 us (8%)
  matrix products  2.33 us (2%)
    all_to_all x1, waiting for transfers between devices, on_device(): lax.all_to_all(state[:, send_perm], 'blk', split_axis=1, concat_axis=1, t...  26.3 us
    all_to_all x1, starting transfers between devices, on_device(): lax.all_to_all(daytime_indicator[:, send_perm], 'blk', split_axis=1, conc...  18.5 us
    all_to_all x1, starting transfers between devices, on_device(): lax.all_to_all(state[:, send_perm], 'blk', split_axis=1, concat_axis=1, t...  12.4 us
    ppermute x2, starting transfers between devices, extended(): after = lax.ppermute(initial, axis, down)  7.39 us
    gather x1, local copies, waits for them, and re-layouts, on_device(): daytime_indicator[:, send_perm]  6.48 us
    ppermute x2, starting transfers between devices, extended(): before = lax.ppermute(last, axis, up)  3.54 us
    gather x1, local copies, waits for them, and re-layouts, on_device(): state[:, send_perm]  3.11 us
    unnamed x22, local copies, waits for them, and re-layouts  2.53 us
  transfers between devices with their start and end apart: 6, of which 1 were waited for; matrix products, arithmetic and copies ran while one was open for 22% of the time, Pallas kernels for 0%

commit v1 on v0

v1 whole, which is shorter than its diff:
```python
import functools
import math

import jax
import jax.numpy as jnp
import numpy as np
from jax import lax
from jax.experimental import pallas as pl
from jax.experimental.pallas import tpu as pltpu
from jax.sharding import PartitionSpec as P

time_step = 0.006
absorb_coef = 0.02
heat_gain = 100.0
sat_base = 3.0
clausius = 0.07
ref_temp = 280.0

MESH = pl.DeviceIdType.MESH
F32, BF16 = jnp.float32, jnp.bfloat16
NZ, NX = 12, 4
NB = NZ * NX
ROWS, LANES, LEV = 16, 128, 32
C = 3 * LEV
CM = C + 8
SITES, PEER = 1152, 24
MSG = 18
KEEP = [ix for ix in range(ROWS) if ix % 4 != 3]


def gll_tables():
    inv_root = 1.0 / math.sqrt(5.0)
    gll_nodes = np.array([-1.0, -inv_root, inv_root, 1.0])
    legendre = (5.0 * gll_nodes**3 - 3.0 * gll_nodes) / 2.0
    deriv_matrix = np.zeros((4, 4))
    for row_index in range(4):
        for col_index in range(4):
            if row_index != col_index:
                deriv_matrix[row_index, col_index] = legendre[row_index] / (
                    legendre[col_index] * (gll_nodes[row_index] - gll_nodes[col_index])
                )
    deriv_matrix[0, 0] = -3.0
    deriv_matrix[3, 3] = 3.0
    weights = np.array([1.0, 5.0, 5.0, 1.0]) / 6.0
    return (deriv_matrix, weights)


DERIV, WEIGHT = gll_tables()


def lane_matrix():
    kron = np.kron(np.eye(LANES // 4), (-WEIGHT[:, None] * DERIV)).T
    hi = kron.astype(jnp.bfloat16).astype(np.float32)
    lo = kron.astype(np.float32) - hi
    full = np.block([[hi, lo], [hi, np.zeros_like(lo)]])
    return full.astype(jnp.bfloat16)


def expand_matrix():
    out = np.zeros((384, 512), np.float32)
    for row in range(4):
        for lane in range(LANES):
            if lane % 4 != 3:
                out[96 * row + 3 * (lane // 4) + lane % 4, 128 * row + lane] = 1.0
    return out.astype(jnp.bfloat16)


def split(x):
    hi = x.astype(BF16)
    return hi, (x - hi.astype(F32)).astype(BF16)


def mm(a, b):
    return jnp.dot(a, b, preferred_element_type=F32)


def step_kernel(
    r_hbm, v_hbm, m_hbm, t_hbm, o_hbm, d_hbm, k_hbm, e_hbm,
    nt_hbm, ph_hbm,
    r_s, v_s, m_s, t_s, o_s, d_s, k_s, e_s,
    w_s, edge_s, hx_s, he_s, nt_s, tg_s, dg_s, oh_s, xt_s, s_s, rc_s, ph_s,
    in_sem, out_sem, hsend, hrecv, ssem, rsem,
):
    f, b = lax.axis_index("face"), lax.axis_index("blk")
    nf = lax.axis_size("face")
    z, x = b // NX, b % NX
    fp, fn = (f + nf - 1) % nf, (f + 1) % nf
    bp, bn = (b + NB - 1) % NB, (b + 1) % NB

    loads = [
        pltpu.make_async_copy(src, dst, in_sem.at[i])
        for i, (src, dst) in enumerate(
            [(r_hbm, r_s), (v_hbm, v_s), (m_hbm, m_s), (k_hbm, k_s), (o_hbm, o_s), (t_hbm, t_s), (d_hbm, d_s), (e_hbm, e_s)]
        )
    ]
    for cp in loads:
        cp.start()

    barrier = pltpu.get_barrier_semaphore()
    halo = [(fp, b), (fn, b), (f, bp), (f, bn), (fp, bp), (fp, bn), (fn, bp), (fn, bn)]

    def greet(i, carry):
        pl.semaphore_signal(barrier, inc=1, device_id=(f, (b + i) % NB), device_id_type=MESH)
        return carry

    lax.fori_loop(1, NB, greet, 0)
    for peer in halo[:2] + halo[4:]:
        pl.semaphore_signal(barrier, inc=1, device_id=peer, device_id_type=MESH)

    lane = lax.broadcasted_iota(jnp.int32, (8, LANES), 1)
    wy = jnp.where((lane % 4 == 0) | (lane % 4 == 3), F32(WEIGHT[0]), F32(WEIGHT[1]))
    for cp in loads[:4]:
        cp.wait()

    for e in range(ROWS // 4):
        fx, fy = [], []
        for i in range(4):
            ix = 4 * e + i
            q = r_s[pl.ds(ix, C, stride=ROWS), :].reshape(3, LEV, LANES)
            met = m_s[ix : ix + 1, :]
            ax = v_s[pl.ds(ix, LEV, stride=ROWS), :] * met
            ay = v_s[pl.ds(LEV * ROWS + ix, LEV, stride=ROWS), :] * met
            fx.append((ax[None] * q).reshape(C, LANES))
            fy.append((ay[None] * q).reshape(C, LANES))
        hi, lo = split(jnp.concatenate(fy, axis=0))
        gy = mm(jnp.concatenate([hi, lo], axis=1), k_s[...])
        gy = gy[:, :LANES] + gy[:, LANES:]
        for i in range(4):
            gx = None
            for j in range(4):
                if DERIV[i, j] != 0.0:
                    term = F32(-WEIGHT[i] * DERIV[i, j]) * fx[j]
                    gx = term if gx is None else gx + term
            w_s[4 * e + i, :C, :] = F32(WEIGHT[i]) * gy[C * i : C * (i + 1)] + wy[:1] * gx
            w_s[4 * e + i, C:, :] = F32(WEIGHT[i]) * wy * m_s[4 * e + i : 4 * e + i + 1, :]

    for e in range(1, ROWS // 4):
        both = w_s[4 * e - 1] + w_s[4 * e]
        w_s[4 * e - 1] = both
        w_s[4 * e] = both
    edge = [jnp.zeros((8, LANES), F32) for _ in range(4)]
    for ix in range(ROWS):
        for v in range(CM // 8):
            g, rv = (v // 3, v % 3) if v < 12 else (0, 3)
            tile = w_s[ix, 8 * v : 8 * v + 8, :]
            moved = pltpu.roll(tile, (1 + 2 * ix + 32 * g) % LANES, 1)
            edge[rv] = jnp.where(lane // 2 == ix + 16 * g, moved, edge[rv])
    for rv in range(4):
        edge_s[8 * rv : 8 * rv + 8, :] = edge[rv]

    pl.semaphore_wait(barrier, NB - 1 + 6)

    def halo_copy(n):
        src = w_s.at[0] if n == 0 else w_s.at[ROWS - 1] if n == 1 else edge_s
        slot = [1, 0, 3, 2, 7, 6, 5, 4][n]
        dst = hx_s.at[slot] if n < 2 else he_s.at[slot - 2]
        return pltpu.make_async_remote_copy(
            src, dst, hsend.at[n], hrecv.at[slot], device_id=halo[n], device_id_type=MESH
        )

    def halo_wait(slot):
        dst = hx_s.at[slot] if slot < 2 else he_s.at[slot - 2]
        pltpu.make_async_remote_copy(
            dst, dst, hsend.at[slot], hrecv.at[slot], device_id=halo[slot], device_id_type=MESH
        ).wait_recv()

    for n in (7, 6, 5, 4, 1, 0, 3, 2):
        halo_copy(n).start()

    for cp in loads[4:]:
        cp.wait()
    warm = [t_s[:, 384 * k : 384 * k + 384] - F32(ref_temp) for k in range(3)]
    warm = jnp.concatenate(warm, axis=0)
    w_hi, w_lo = split(warm)
    w_lo2 = (warm - w_hi.astype(F32) - w_lo.astype(F32)).astype(BF16)
    day = [jnp.broadcast_to(d_s[:, 384 * k : 384 * k + 384].astype(F32), (16, 384)) for k in range(3)]
    day = jnp.concatenate(day, axis=0).astype(BF16)
    grid = mm(jnp.concatenate([w_hi, w_lo, w_lo2, day], axis=0), e_s[...])
    heat = grid[:C] + grid[C : 2 * C] + grid[2 * C : 3 * C] + F32(ref_temp)
    for k in range(3):
        for i in range(4):
            tg_s[4 * k + i] = heat[LEV * k : LEV * (k + 1), LANES * i : LANES * (i + 1)]
            dg_s[4 * k + i] = grid[3 * C + 16 * k : 3 * C + 16 * k + 8, LANES * i : LANES * (i + 1)]

    site = jnp.where(lane % 4 == 3, -4096, 3 * (lane // 4) + lane % 4)[:1]
    for k in range(SITES // LANES):
        want = jnp.broadcast_to(o_s[:, LANES * k : LANES * (k + 1)], (LANES, LANES)).T
        for j in range(12):
            oh_s[LANES * k : LANES * (k + 1), LANES * j : LANES * (j + 1)] = jnp.where(
                want == site + 96 * j, F32(1.0), F32(0.0)
            ).astype(BF16)

    for slot in range(8):
        halo_wait(slot)

    pos = lane % 32
    add = []
    for rv in range(4):
        rows = pl.ds(8 * rv, 8)
        prev, nxt = he_s[0, rows, :], he_s[1, rows, :]
        c = jnp.where(pos % 2 == 1, pltpu.roll(prev, 1, 1), pltpu.roll(nxt, LANES - 1, 1))
        pp, pn, np_, nn = [he_s[2 + n, rows, :] for n in range(4)]
        zero = jnp.zeros_like(c)
        c = c + jnp.where(pos == 1, pltpu.roll(pp, LANES - 29, 1), zero)
        c = c + jnp.where(pos == 0, pltpu.roll(pn, LANES - 31, 1), zero)
        c = c + jnp.where(pos == 31, pltpu.roll(np_, 31, 1), zero)
        c = c + jnp.where(pos == 30, pltpu.roll(nn, 29, 1), zero)
        add.append(c)

    def finish_row(ix):
        tiles = []
        for v in range(CM // 8):
            g, rv = (v // 3, v % 3) if v < 12 else (0, 3)
            s = w_s[ix, 8 * v : 8 * v + 8, :]
            if ix == 0:
                s = s + hx_s[0, 8 * v : 8 * v + 8, :]
            if ix == ROWS - 1:
                s = s + hx_s[1, 8 * v : 8 * v + 8, :]
            far = pltpu.roll(add[rv], (2 * LANES - (2 * ix + 1 + 32 * g)) % LANES, 1)
            other = jnp.where(
                lane % 4 == 3,
                pltpu.roll(s, LANES - 1, 1),
                jnp.where(lane % 4 == 0, pltpu.roll(s, 1, 1), F32(0.0)),
            )
            other = jnp.where((lane == 0) | (lane == LANES - 1), far, other)
            tiles.append(s + other)
        rate = F32(time_step) / tiles[12]
        q = r_s[pl.ds(ix, C, stride=ROWS), :]
        new = q + jnp.concatenate([t * rate for t in tiles[:12]], axis=0)
        nt_s[pl.ds(ix, C, stride=ROWS), :] = new
        return new

    level = lax.broadcasted_iota(jnp.int32, (LEV, LANES), 0)

    def physics(j, new):
        vapour, heavy, deuter = new[:LEV], new[LEV : 2 * LEV], new[2 * LEV :]
        depth = F32(absorb_coef) * vapour
        for shift in (1, 2, 4, 8, 16):
            depth = depth + jnp.where(level >= shift, pltpu.roll(depth, shift, 0), F32(0.0))
        heating = F32(heat_gain * absorb_coef) * vapour * jnp.exp(-depth)
        warmed = tg_s[j] + jnp.where(dg_s[j][:1] == 1.0, heating, F32(0.0))
        saturation = F32(sat_base) * jnp.exp(F32(clausius) * (warmed - F32(ref_temp)))
        remain = jnp.minimum(vapour, saturation)
        log_ratio = jnp.log(remain / vapour)
        inverse = 1.0 / warmed
        alpha_heavy = jnp.exp(F32(1137.0) * inverse * inverse - F32(0.4156) * inverse - F32(0.0020667))
        alpha_deut = jnp.exp(F32(24844.0) * inverse * inverse - F32(76.248) * inverse + F32(0.052612))
        out = [remain, heavy * jnp.exp(alpha_heavy * log_ratio), deuter * jnp.exp(alpha_deut * log_ratio)]
        out = jnp.concatenate(out + [jnp.zeros((LEV, LANES), F32)], axis=0).T
        hi, lo = split(out)
        xt_s[LANES * j : LANES * (j + 1), :LANES] = hi
        xt_s[LANES * j : LANES * (j + 1), LANES:] = lo

    for j, ix in enumerate(KEEP):
        physics(j, finish_row(ix))

    row8 = lax.broadcasted_iota(jnp.int32, (1, 8, LANES), 1)
    lane8 = lax.broadcasted_iota(jnp.int32, (1, 8, LANES), 2)
    top, late = row8 >= 2, lane8 >= C

    def send_copy(p, slot):
        return pltpu.make_async_remote_copy(
            s_s.at[p], rc_s.at[slot], ssem.at[p], rsem.at[slot], device_id=(f, p), device_id_type=MESH
        )

    def send(n, carry):
        k = 6 - n
        zs = [(z + k) % NZ, (z + NZ + 1 - k) % NZ]
        lhs = [oh_s[pl.ds(pl.multiple_of(zz * 96, 96), 96), :] for zz in zs]
        y = mm(jnp.concatenate(lhs, axis=0), xt_s[...])
        y = (y[:, :LANES] + y[:, LANES:]).reshape(8, PEER, LANES)
        v0, v1, v2 = y[:, 0:8], y[:, 8:16], y[:, 16:24]
        a0, a1, a2 = pltpu.roll(v2, 96, 2), pltpu.roll(v2, 64, 2), pltpu.roll(v2, 32, 2)
        v0 = jnp.where(late, jnp.where(top, a0, pltpu.roll(a2, 6, 1)), v0)
        v1 = jnp.where(late, jnp.where(top, a1, pltpu.roll(a2, 4, 1)), v1)
        v2 = jnp.where(late, pltpu.roll(a2, 2, 1), v2)
        for h in range(2):
            rows = pl.ds(zs[h] * NX, NX)
            s_s[rows, 0:8, :] = v0[4 * h : 4 * h + 4]
            s_s[rows, 8:16, :] = v1[4 * h : 4 * h + 4]
            s_s[rows, 16:18, :] = v2[4 * h : 4 * h + 4, 0:2]
        for h in range(2):
            for xx in range(NX):
                p = zs[h] * NX + (x + xx) % NX

                @pl.when(p != b)
                def _():
                    send_copy(p, b).start()

        return carry

    lax.fori_loop(0, NZ // 2, send, 0)
    rc_s[b] = s_s[b]

    for ix in range(3, ROWS, 4):
        finish_row(ix)
    out_nt = pltpu.make_async_copy(nt_s, nt_hbm, out_sem.at[0])
    out_nt.start()
    for n in range(8):
        halo_copy(n).wait_send()

    outs = []
    for g in range(3):
        def arrive(i, carry):
            p = 16 * g + i

            @pl.when(p != b)
            def _():
                send_copy(p, p).wait_recv()

            return carry

        lax.fori_loop(0, 16, arrive, 0)
        grp = pl.ds(16 * g, 16)
        v0, v1 = rc_s[grp, 0:8, :], rc_s[grp, 8:16, :]
        v2 = jnp.concatenate([rc_s[grp, 16:18, :], jnp.zeros((16, 6, LANES), F32)], axis=1)
        a2 = jnp.where(
            row8 < 4, pltpu.roll(v0, 2, 1), jnp.where(row8 < 6, pltpu.roll(v1, 4, 1), pltpu.roll(v2, 6, 1))
        )
        tail = jnp.where(
            lane8 < 32, pltpu.roll(v0, 32, 2), jnp.where(lane8 < 64, pltpu.roll(v1, 64, 2), pltpu.roll(a2, 96, 2))
        )
        v2 = jnp.where(top, tail, v2)
        cols = jnp.concatenate([v0, v1, v2], axis=1).reshape(16 * PEER, LANES)
        ph_s[:, 384 * g : 384 * (g + 1)] = cols.T[:C]
        outs.append(
            pltpu.make_async_copy(
                ph_s.at[:, pl.ds(384 * g, 384)], ph_hbm.at[:, pl.ds(384 * g, 384)], out_sem.at[1 + g]
            )
        )
        outs[-1].start()

    def drain(i, carry):
        @pl.when(i != b)
        def _():
            send_copy(i, b).wait_send()

        return carry

    lax.fori_loop(0, NB, drain, 0)
    for cp in [out_nt] + outs:
        cp.wait()


def on_device(isotope_ratios, advecting_velocity, metric_scaling, thermal_state, outgoing_site_order, daytime_indicator):
    hbm = pl.BlockSpec(memory_space=pltpu.HBM)
    vm = lambda *shape, dtype=F32: pltpu.VMEM(shape, dtype)
    new_tracers, physics = pl.pallas_call(
        step_kernel,
        out_shape=(
            jax.ShapeDtypeStruct((C * ROWS, LANES), F32),
            jax.ShapeDtypeStruct((C, SITES), F32),
        ),
        in_specs=[hbm] * 8,
        out_specs=(hbm, hbm),
        scratch_shapes=[
            vm(C * ROWS, LANES), vm(2 * LEV * ROWS, LANES), vm(ROWS, LANES), vm(LEV, SITES),
            vm(1, SITES, dtype=jnp.int32), vm(1, SITES, dtype=jnp.int32),
            vm(2 * LANES, 2 * LANES, dtype=BF16), vm(384, 512, dtype=BF16),
            vm(ROWS, CM, LANES), vm(LEV, LANES), vm(2, CM, LANES), vm(6, LEV, LANES),
            vm(C * ROWS, LANES), vm(12, LEV, LANES), vm(12, 8, LANES),
            vm(SITES, 12 * LANES, dtype=BF16), vm(12 * LANES, 2 * LANES, dtype=BF16),
            vm(NB, MSG, LANES), vm(NB, MSG, LANES), vm(C, SITES),
            pltpu.SemaphoreType.DMA((8,)), pltpu.SemaphoreType.DMA((4,)),
            pltpu.SemaphoreType.DMA((8,)), pltpu.SemaphoreType.DMA((8,)),
            pltpu.SemaphoreType.DMA((NB,)), pltpu.SemaphoreType.DMA((NB,)),
        ],
        compiler_params=pltpu.CompilerParams(
            collective_id=0, has_side_effects=True, vmem_limit_bytes=48 * 1024 * 1024
        ),
        name="transport_condense",
    )(
        isotope_ratios.reshape(C * ROWS, LANES),
        advecting_velocity.reshape(2 * LEV * ROWS, LANES),
        metric_scaling,
        thermal_state[0],
        outgoing_site_order,
        daytime_indicator,
        jnp.asarray(lane_matrix()),
        jnp.asarray(expand_matrix()),
    )
    return (new_tracers.reshape(3, LEV, ROWS, LANES), physics.reshape(1, 3, LEV, SITES))


def solution(mesh):
    placed = (
        P(None, None, "face", "blk"),
        P(None, None, "face", "blk"),
        P("face", "blk"),
        P("face", None, "blk"),
        P("face", "blk"),
        P("face", "blk"),
    )
    return jax.shard_map(
        on_device,
        mesh=mesh,
        in_specs=placed,
        out_specs=(P(None, None, "face", "blk"), P("face", None, None, "blk")),
        check_vma=False,
    )
```

time: 102 us -> 54.3 us (0.53)
  the two profiles are of different devices: /device:TPU:24 before, /device:TPU:1 now
where the time goes in v1:
time: 54.3 us; the launch traced here: 53.9 us
  Pallas kernels  44.5 us (82%)
  local copies, waits for them, and re-layouts  8.69 us (16%)
  between operations  0.66 us (1%)
    pallas_call x1, Pallas kernels, on_device(): pl.pallas_call(step_kernel, out_shape=(jax.ShapeDtypeStruct((C * ROWS, LA...  44.5 us
    unnamed x18, local copies, waits for them, and re-layouts  8.69 us

profile of v1, /device:TPU:1, one launch (start us, length us, event | category | flops | bytes accessed | tf_op | source)
XLA Modules:
  0.0 53.9 jit_solution(15508603344212411428)
XLA Ops:
  0.6 0.0 copy-start.6
  0.6 0.7 %copy-done.6 = s32[1,1152]{1,0:T(1,128)S(1)} copy-done((s32[1,1152]{1,0:T(1,128)S(1)}, s32[1,1152]{1,0:T(1,128)}, u32[]{:S(2)}) %copy-start.6) | copy-done | bytes 4632
  1.3 0.0 copy-start
  1.3 1.1 %copy-done = f32[3,32,16,128]{3,2,1,0:T(8,128)S(1)} copy-done((f32[3,32,16,128]{3,2,1,0:T(8,128)S(1)}, f32[3,32,16,128]{3,2,1,0:T(8,128)}, u32[]{:S(2)}) %copy-start) | copy-done | bytes 786456
  2.5 0.0 copy-start.1
  2.5 1.0 %copy-done.1 = f32[2,32,16,128]{3,2,1,0:T(8,128)S(1)} copy-done((f32[2,32,16,128]{3,2,1,0:T(8,128)S(1)}, f32[2,32,16,128]{3,2,1,0:T(8,128)}, u32[]{:S(2)}) %copy-start.1) | copy-done | bytes 524312
  3.5 0.0 copy-start.2
  3.5 1.0 %copy-done.2 = bf16[384,512]{1,0:T(8,128)(2,1)S(1)} copy-done((bf16[384,512]{1,0:T(8,128)(2,1)S(1)}, bf16[384,512]{1,0:T(8,128)(2,1)}, u32[]{:S(2)}) %copy-start.2) | copy-done | bytes 393240
  4.5 0.0 copy-start.3
  4.5 0.9 %copy-done.3 = f32[1,32,1152]{2,1,0:T(8,128)S(1)} copy-done((f32[1,32,1152]{2,1,0:T(8,128)S(1)}, f32[1,32,1152]{2,1,0:T(8,128)}, u32[]{:S(2)}) %copy-start.3) | copy-done | bytes 147480
  5.4 0.0 copy-start.4
  5.4 0.9 %copy-done.4 = bf16[256,256]{1,0:T(8,128)(2,1)S(1)} copy-done((bf16[256,256]{1,0:T(8,128)(2,1)S(1)}, bf16[256,256]{1,0:T(8,128)(2,1)}, u32[]{:S(2)}) %copy-start.4) | copy-done | bytes 131096
  6.3 0.0 copy-start.5
  6.3 0.7 %copy-done.5 = f32[16,128]{1,0:T(8,128)S(1)} copy-done((f32[16,128]{1,0:T(8,128)S(1)}, f32[16,128]{1,0:T(8,128)}, u32[]{:S(2)}) %copy-start.5) | copy-done | bytes 8216
  7.0 0.0 copy-start.7
  7.0 0.7 %copy-done.7 = s32[1,1152]{1,0:T(1,128)S(1)} copy-done((s32[1,1152]{1,0:T(1,128)S(1)}, s32[1,1152]{1,0:T(1,128)}, u32[]{:S(2)}) %copy-start.7) | copy-done | bytes 4632
  7.7 44.5 %transport_condense.1 = (f32[1536,128]{1,0:T(8,128)S(1)}, f32[96,1152]{1,0:T(8,128)S(1)}) custom-call(f32[1536,128]{1,0:T(8,128)S(1)} %bitcast.5, f32[1024,128]{1,0:T(8,128)S(1)} %bitcast.7, f32[16,128]{1,0:T(8,128)S(1)} %copy-done.5, f32[32,1152]{1,0:T(8,128)S(1)} %bitcast.9, s32[1,1152]{1,0:T(1,128)S(1)} %copy-done.6, s32[1,1152]{1,0:T(1,128)S(1)} %copy-done.7, ...), custom_call_target="tpu_custom_call" | custom-call | tf_op jit(solution)/shard_map/transport_condense/pallas_call | solution.py:348
  52.2 0.9 %copy.12 = f32[3,32,16,128]{3,2,1,0:T(8,128)} copy(f32[3,32,16,128]{3,2,1,0:T(8,128)S(1)} %bitcast.6) | data formatting | bytes 1572864
  53.1 0.8 %copy.13 = f32[1,3,32,1152]{3,2,1,0:T(8,128)} copy(f32[1,3,32,1152]{3,2,1,0:T(8,128)S(1)} %bitcast.8) | data formatting | bytes 884736
Async XLA Ops:
  0.6 0.7 %copy-start.6 = (s32[1,1152]{1,0:T(1,128)S(1)}, s32[1,1152]{1,0:T(1,128)}, u32[]{:S(2)}) copy-start(s32[1,1152]{1,0:T(1,128)} %o_hbm.1) | copy-start | bytes 13828
  1.3 1.1 %copy-start = (f32[3,32,16,128]{3,2,1,0:T(8,128)S(1)}, f32[3,32,16,128]{3,2,1,0:T(8,128)}, u32[]{:S(2)}) copy-start(f32[3,32,16,128]{3,2,1,0:T(8,128)} %param.8) | copy-start | bytes 2359300
  2.5 1.0 %copy-start.1 = (f32[2,32,16,128]{3,2,1,0:T(8,128)S(1)}, f32[2,32,16,128]{3,2,1,0:T(8,128)}, u32[]{:S(2)}) copy-start(f32[2,32,16,128]{3,2,1,0:T(8,128)} %param.9) | copy-start | bytes 1572868
  3.5 1.0 %copy-start.2 = (bf16[384,512]{1,0:T(8,128)(2,1)S(1)}, bf16[384,512]{1,0:T(8,128)(2,1)}, u32[]{:S(2)}) copy-start(bf16[384,512]{1,0:T(8,128)(2,1)} %constant.5.clone.e_hbm) | copy-start | bytes 1179652
  4.5 0.9 %copy-start.3 = (f32[1,32,1152]{2,1,0:T(8,128)S(1)}, f32[1,32,1152]{2,1,0:T(8,128)}, u32[]{:S(2)}) copy-start(f32[1,32,1152]{2,1,0:T(8,128)} %param.11) | copy-start | bytes 442372
  5.4 0.9 %copy-start.4 = (bf16[256,256]{1,0:T(8,128)(2,1)S(1)}, bf16[256,256]{1,0:T(8,128)(2,1)}, u32[]{:S(2)}) copy-start(bf16[256,256]{1,0:T(8,128)(2,1)} %constant.4.clone.k_hbm) | copy-start | bytes 393220
  6.3 0.7 %copy-start.5 = (f32[16,128]{1,0:T(8,128)S(1)}, f32[16,128]{1,0:T(8,128)}, u32[]{:S(2)}) copy-start(f32[16,128]{1,0:T(8,128)} %m_hbm.1) | copy-start | bytes 24580
  7.0 0.7 %copy-start.7 = (s32[1,1152]{1,0:T(1,128)S(1)}, s32[1,1152]{1,0:T(1,128)}, u32[]{:S(2)}) copy-start(s32[1,1152]{1,0:T(1,128)} %d_hbm.1) | copy-start | bytes 13828

commit v2 on v1

--- a/solution.py
+++ b/solution.py
@@ -25,6 +25,7 @@
 CM = C + 8
 SITES, PEER = 1152, 24
 MSG = 18
+GRANT = 67043328
 KEEP = [ix for ix in range(ROWS) if ix % 4 != 3]
 
 
@@ -76,10 +77,10 @@
 
 def step_kernel(
     r_hbm, v_hbm, m_hbm, t_hbm, o_hbm, d_hbm, k_hbm, e_hbm,
-    nt_hbm, ph_hbm,
+    nt_s, rc_s,
     r_s, v_s, m_s, t_s, o_s, d_s, k_s, e_s,
-    w_s, edge_s, hx_s, he_s, nt_s, tg_s, dg_s, oh_s, xt_s, s_s, rc_s, ph_s,
-    in_sem, out_sem, hsend, hrecv, ssem, rsem,
+    w_s, edge_s, hx_s, he_s, tg_s, dg_s, oh_s, xt_s, s_s,
+    in_sem, hsend, hrecv, ssem, rsem, round_sem,
 ):
     f, b = lax.axis_index("face"), lax.axis_index("blk")
     nf = lax.axis_size("face")
@@ -96,16 +97,17 @@
     for cp in loads:
         cp.start()
 
+    halo = [(fp, b), (fn, b), (f, bp), (f, bn), (fp, bp), (fp, bn), (fn, bp), (fn, bn)]
+    row_mates = [(f, z * NX + (x + d) % NX) for d in range(1, NX)]
+    column_mates = [(f, (z + d) % NZ * NX + x) for d in (1, NZ - 1, 2, NZ - 2, 3, NZ - 3)]
+
+    def greet(sem, peers):
+        for peer in peers:
+            pl.semaphore_signal(sem, inc=1, device_id=peer, device_id_type=MESH)
+
     barrier = pltpu.get_barrier_semaphore()
-    halo = [(fp, b), (fn, b), (f, bp), (f, bn), (fp, bp), (fp, bn), (fn, bp), (fn, bn)]
-
-    def greet(i, carry):
-        pl.semaphore_signal(barrier, inc=1, device_id=(f, (b + i) % NB), device_id_type=MESH)
-        return carry
-
-    lax.fori_loop(1, NB, greet, 0)
-    for peer in halo[:2] + halo[4:]:
-        pl.semaphore_signal(barrier, inc=1, device_id=peer, device_id_type=MESH)
+    near = column_mates[::-1] + halo + row_mates
+    greet(barrier, near)
 
     lane = lax.broadcasted_iota(jnp.int32, (8, LANES), 1)
     wy = jnp.where((lane % 4 == 0) | (lane % 4 == 3), F32(WEIGHT[0]), F32(WEIGHT[1]))
@@ -148,7 +150,8 @@
     for rv in range(4):
         edge_s[8 * rv : 8 * rv + 8, :] = edge[rv]
 
-    pl.semaphore_wait(barrier, NB - 1 + 6)
+    pl.semaphore_wait(barrier, len(near))
+    greet(round_sem.at[0], column_mates[::-1] + row_mates)
 
     def halo_copy(n):
         src = w_s.at[0] if n == 0 else w_s.at[ROWS - 1] if n == 1 else edge_s
@@ -190,6 +193,8 @@
                 want == site + 96 * j, F32(1.0), F32(0.0)
             ).astype(BF16)
 
+    pl.semaphore_wait(round_sem.at[0], len(column_mates) + len(row_mates))
+    greet(round_sem.at[1], row_mates)
     for slot in range(8):
         halo_wait(slot)
 
@@ -289,28 +294,33 @@
 
         return carry
 
+    pl.semaphore_wait(round_sem.at[1], len(row_mates))
     lax.fori_loop(0, NZ // 2, send, 0)
     rc_s[b] = s_s[b]
 
     for ix in range(3, ROWS, 4):
         finish_row(ix)
-    out_nt = pltpu.make_async_copy(nt_s, nt_hbm, out_sem.at[0])
-    out_nt.start()
     for n in range(8):
         halo_copy(n).wait_send()
 
+    def arrive(i, carry):
+        @pl.when(i != b)
+        def _():
+            send_copy(i, b).wait_send()
+            send_copy(i, i).wait_recv()
+
+        return carry
+
+    lax.fori_loop(0, NB, arrive, 0)
+
+
+def write_kernel(nt_s, rc_s, nt_hbm, ph_hbm, ph_s, sem):
+    out_nt = pltpu.make_async_copy(nt_s, nt_hbm, sem.at[0])
+    out_nt.start()
+    row8 = lax.broadcasted_iota(jnp.int32, (1, 8, LANES), 1)
+    lane8 = lax.broadcasted_iota(jnp.int32, (1, 8, LANES), 2)
     outs = []
     for g in range(3):
-        def arrive(i, carry):
-            p = 16 * g + i
-
-            @pl.when(p != b)
-            def _():
-                send_copy(p, p).wait_recv()
-
-            return carry
-
-        lax.fori_loop(0, 16, arrive, 0)
         grp = pl.ds(16 * g, 16)
         v0, v1 = rc_s[grp, 0:8, :], rc_s[grp, 8:16, :]
         v2 = jnp.concatenate([rc_s[grp, 16:18, :], jnp.zeros((16, 6, LANES), F32)], axis=1)
@@ -320,24 +330,12 @@
         tail = jnp.where(
             lane8 < 32, pltpu.roll(v0, 32, 2), jnp.where(lane8 < 64, pltpu.roll(v1, 64, 2), pltpu.roll(a2, 96, 2))
         )
-        v2 = jnp.where(top, tail, v2)
+        v2 = jnp.where(row8 >= 2, tail, v2)
         cols = jnp.concatenate([v0, v1, v2], axis=1).reshape(16 * PEER, LANES)
-        ph_s[:, 384 * g : 384 * (g + 1)] = cols.T[:C]
-        outs.append(
-            pltpu.make_async_copy(
-                ph_s.at[:, pl.ds(384 * g, 384)], ph_hbm.at[:, pl.ds(384 * g, 384)], out_sem.at[1 + g]
-            )
-        )
+        part = pl.ds(384 * g, 384)
+        ph_s[:, part] = cols.T[:C]
+        outs.append(pltpu.make_async_copy(ph_s.at[:, part], ph_hbm.at[:, part], sem.at[1 + g]))
         outs[-1].start()
-
-    def drain(i, carry):
-        @pl.when(i != b)
-        def _():
-            send_copy(i, b).wait_send()
-
-        return carry
-
-    lax.fori_loop(0, NB, drain, 0)
     for cp in [out_nt] + outs:
         cp.wait()
 
@@ -345,28 +343,27 @@
 def on_device(isotope_ratios, advecting_velocity, metric_scaling, thermal_state, outgoing_site_order, daytime_indicator):
     hbm = pl.BlockSpec(memory_space=pltpu.HBM)
     vm = lambda *shape, dtype=F32: pltpu.VMEM(shape, dtype)
-    new_tracers, physics = pl.pallas_call(
+    moved = (vm(C * ROWS, LANES), vm(NB, MSG, LANES))
+    new_tracers, arrived = pl.pallas_call(
         step_kernel,
-        out_shape=(
-            jax.ShapeDtypeStruct((C * ROWS, LANES), F32),
-            jax.ShapeDtypeStruct((C, SITES), F32),
-        ),
+        out_shape=moved,
         in_specs=[hbm] * 8,
-        out_specs=(hbm, hbm),
+        out_specs=(pl.BlockSpec(memory_space=pltpu.VMEM),) * 2,
         scratch_shapes=[
             vm(C * ROWS, LANES), vm(2 * LEV * ROWS, LANES), vm(ROWS, LANES), vm(LEV, SITES),
             vm(1, SITES, dtype=jnp.int32), vm(1, SITES, dtype=jnp.int32),
             vm(2 * LANES, 2 * LANES, dtype=BF16), vm(384, 512, dtype=BF16),
             vm(ROWS, CM, LANES), vm(LEV, LANES), vm(2, CM, LANES), vm(6, LEV, LANES),
-            vm(C * ROWS, LANES), vm(12, LEV, LANES), vm(12, 8, LANES),
+            vm(12, LEV, LANES), vm(12, 8, LANES),
             vm(SITES, 12 * LANES, dtype=BF16), vm(12 * LANES, 2 * LANES, dtype=BF16),
-            vm(NB, MSG, LANES), vm(NB, MSG, LANES), vm(C, SITES),
-            pltpu.SemaphoreType.DMA((8,)), pltpu.SemaphoreType.DMA((4,)),
+            vm(NB, MSG, LANES),
+            pltpu.SemaphoreType.DMA((8,)),
             pltpu.SemaphoreType.DMA((8,)), pltpu.SemaphoreType.DMA((8,)),
             pltpu.SemaphoreType.DMA((NB,)), pltpu.SemaphoreType.DMA((NB,)),
+            pltpu.SemaphoreType.REGULAR((2,)),
         ],
         compiler_params=pltpu.CompilerParams(
-            collective_id=0, has_side_effects=True, vmem_limit_bytes=48 * 1024 * 1024
+            collective_id=0, has_side_effects=True, vmem_limit_bytes=GRANT - 1536 * 1024
         ),
         name="transport_condense",
     )(
@@ -379,6 +376,18 @@
         jnp.asarray(lane_matrix()),
         jnp.asarray(expand_matrix()),
     )
+    new_tracers, physics = pl.pallas_call(
+        write_kernel,
+        out_shape=(
+            jax.ShapeDtypeStruct((C * ROWS, LANES), F32),
+            jax.ShapeDtypeStruct((C, SITES), F32),
+        ),
+        in_specs=(pl.BlockSpec(memory_space=pltpu.VMEM),) * 2,
+        out_specs=(hbm, hbm),
+        scratch_shapes=[vm(C, SITES), pltpu.SemaphoreType.DMA((4,))],
+        compiler_params=pltpu.CompilerParams(vmem_limit_bytes=8 * 1024 * 1024),
+        name="write_results",
+    )(new_tracers, arrived)
     return (new_tracers.reshape(3, LEV, ROWS, LANES), physics.reshape(1, 3, LEV, SITES))
 
 

time: 54.3 us -> 44.3 us (0.82)
  local copies, waits for them, and re-layouts: 8.69 us -> 0 us
  Pallas kernels: 44.5 us -> 43.5 us
    unnamed x18 -> x0, local copies, waits for them, and re-layouts: 8.69 us -> none
    pallas_call x1 -> x2, Pallas kernels: 44.5 us -> 43.5 us  [the longest x1 42.4 us: on_device(): pl.pallas_call(step_kernel, out_shape=moved, in_specs=[hbm] * 8, out_spec...]
where the time goes in v2:
time: 44.3 us; the launch traced here: 44.1 us
  Pallas kernels  43.5 us (98%)
  between operations  0.64 us (1%)
    pallas_call x1, Pallas kernels, on_device(): pl.pallas_call(step_kernel, out_shape=moved, in_specs=[hbm] * 8, out_spec...  42.4 us
    pallas_call x1, Pallas kernels, on_device(): pl.pallas_call(write_kernel, out_shape=(jax.ShapeDtypeStruct((C * ROWS, L...  1.09 us

profile of v2, /device:TPU:1, one launch (start us, length us, event | category | flops | bytes accessed | tf_op | source)
XLA Modules:
  0.0 44.1 jit_solution(5724800573370238845)
XLA Ops:
  0.6 42.4 %transport_condense.1 = (f32[1536,128]{1,0:T(8,128)S(1)}, f32[48,18,128]{2,1,0:T(8,128)S(1)}) custom-call(f32[1536,128]{1,0:T(8,128)} %bitcast.5, f32[1024,128]{1,0:T(8,128)} %bitcast.6, f32[16,128]{1,0:T(8,128)} %m_hbm.1, f32[32,1152]{1,0:T(8,128)} %bitcast.7, s32[1,1152]{1,0:T(1,128)} %o_hbm.1, s32[1,1152]{1,0:T(1,128)} %d_hbm.1, ...), custom_call_target="tpu_custom_call" | custom-call | tf_op jit(solution)/shard_map/transport_condense/pallas_call | solution.py:347
  43.0 1.1 %write_results.1 = (f32[1536,128]{1,0:T(8,128)}, f32[96,1152]{1,0:T(8,128)}) custom-call(f32[1536,128]{1,0:T(8,128)S(1)} %get-tuple-element.6.nt_s, f32[48,18,128]{2,1,0:T(8,128)S(1)} %get-tuple-element.7.rc_s), custom_call_target="tpu_custom_call" | custom-call | tf_op jit(solution)/shard_map/write_results/pallas_call | solution.py:379

commit v3 on v2

--- a/solution.py
+++ b/solution.py
@@ -151,7 +151,8 @@
         edge_s[8 * rv : 8 * rv + 8, :] = edge[rv]
 
     pl.semaphore_wait(barrier, len(near))
-    greet(round_sem.at[0], column_mates[::-1] + row_mates)
+    greet(round_sem.at[1], column_mates[4:])
+    greet(round_sem.at[0], row_mates)
 
     def halo_copy(n):
         src = w_s.at[0] if n == 0 else w_s.at[ROWS - 1] if n == 1 else edge_s
@@ -167,7 +168,7 @@
             dst, dst, hsend.at[slot], hrecv.at[slot], device_id=halo[slot], device_id_type=MESH
         ).wait_recv()
 
-    for n in (7, 6, 5, 4, 1, 0, 3, 2):
+    for n in (7, 1, 3, 6, 5, 4, 0, 2):
         halo_copy(n).start()
 
     for cp in loads[4:]:
@@ -193,26 +194,29 @@
                 want == site + 96 * j, F32(1.0), F32(0.0)
             ).astype(BF16)
 
-    pl.semaphore_wait(round_sem.at[0], len(column_mates) + len(row_mates))
-    greet(round_sem.at[1], row_mates)
-    for slot in range(8):
+    pl.semaphore_wait(round_sem.at[1], 2)
+    greet(round_sem.at[2], row_mates)
+    for slot in (0, 2, 4):
         halo_wait(slot)
 
     pos = lane % 32
-    add = []
-    for rv in range(4):
-        rows = pl.ds(8 * rv, 8)
-        prev, nxt = he_s[0, rows, :], he_s[1, rows, :]
-        c = jnp.where(pos % 2 == 1, pltpu.roll(prev, 1, 1), pltpu.roll(nxt, LANES - 1, 1))
-        pp, pn, np_, nn = [he_s[2 + n, rows, :] for n in range(4)]
-        zero = jnp.zeros_like(c)
-        c = c + jnp.where(pos == 1, pltpu.roll(pp, LANES - 29, 1), zero)
-        c = c + jnp.where(pos == 0, pltpu.roll(pn, LANES - 31, 1), zero)
-        c = c + jnp.where(pos == 31, pltpu.roll(np_, 31, 1), zero)
-        c = c + jnp.where(pos == 30, pltpu.roll(nn, 29, 1), zero)
-        add.append(c)
-
-    def finish_row(ix):
+
+    def edge_lanes(whole):
+        add = []
+        for rv in range(4):
+            rows = pl.ds(8 * rv, 8)
+            before = pltpu.roll(he_s[0, rows, :], 1, 1)
+            before = before + jnp.where(pos == 1, pltpu.roll(he_s[2, rows, :], LANES - 29, 1), F32(0.0))
+            after = jnp.zeros_like(before)
+            if whole:
+                after = pltpu.roll(he_s[1, rows, :], LANES - 1, 1)
+                before = before + jnp.where(pos == 31, pltpu.roll(he_s[4, rows, :], 31, 1), F32(0.0))
+                after = after + jnp.where(pos == 0, pltpu.roll(he_s[3, rows, :], LANES - 31, 1), F32(0.0))
+                after = after + jnp.where(pos == 30, pltpu.roll(he_s[5, rows, :], 29, 1), F32(0.0))
+            add.append(jnp.where(pos % 2 == 1, before, after))
+        return add
+
+    def finish_row(ix, add):
         tiles = []
         for v in range(CM // 8):
             g, rv = (v // 3, v % 3) if v < 12 else (0, 3)
@@ -231,9 +235,7 @@
             tiles.append(s + other)
         rate = F32(time_step) / tiles[12]
         q = r_s[pl.ds(ix, C, stride=ROWS), :]
-        new = q + jnp.concatenate([t * rate for t in tiles[:12]], axis=0)
-        nt_s[pl.ds(ix, C, stride=ROWS), :] = new
-        return new
+        return q + jnp.concatenate([t * rate for t in tiles[:12]], axis=0)
 
     level = lax.broadcasted_iota(jnp.int32, (LEV, LANES), 0)
 
@@ -256,8 +258,9 @@
         xt_s[LANES * j : LANES * (j + 1), :LANES] = hi
         xt_s[LANES * j : LANES * (j + 1), LANES:] = lo
 
+    add = edge_lanes(False)
     for j, ix in enumerate(KEEP):
-        physics(j, finish_row(ix))
+        physics(j, finish_row(ix, add))
 
     row8 = lax.broadcasted_iota(jnp.int32, (1, 8, LANES), 1)
     lane8 = lax.broadcasted_iota(jnp.int32, (1, 8, LANES), 2)
@@ -268,10 +271,8 @@
             s_s.at[p], rc_s.at[slot], ssem.at[p], rsem.at[slot], device_id=(f, p), device_id_type=MESH
         )
 
-    def send(n, carry):
-        k = 6 - n
-        zs = [(z + k) % NZ, (z + NZ + 1 - k) % NZ]
-        lhs = [oh_s[pl.ds(pl.multiple_of(zz * 96, 96), 96), :] for zz in zs]
+    def send(rows_of_z):
+        lhs = [oh_s[pl.ds(pl.multiple_of(zz * 96, 96), 96), :] for zz in rows_of_z]
         y = mm(jnp.concatenate(lhs, axis=0), xt_s[...])
         y = (y[:, :LANES] + y[:, LANES:]).reshape(8, PEER, LANES)
         v0, v1, v2 = y[:, 0:8], y[:, 8:16], y[:, 16:24]
@@ -280,26 +281,36 @@
         v1 = jnp.where(late, jnp.where(top, a1, pltpu.roll(a2, 4, 1)), v1)
         v2 = jnp.where(late, pltpu.roll(a2, 2, 1), v2)
         for h in range(2):
-            rows = pl.ds(zs[h] * NX, NX)
+            rows = pl.ds(rows_of_z[h] * NX, NX)
             s_s[rows, 0:8, :] = v0[4 * h : 4 * h + 4]
             s_s[rows, 8:16, :] = v1[4 * h : 4 * h + 4]
             s_s[rows, 16:18, :] = v2[4 * h : 4 * h + 4, 0:2]
         for h in range(2):
             for xx in range(NX):
-                p = zs[h] * NX + (x + xx) % NX
+                p = rows_of_z[h] * NX + (x + xx) % NX
 
                 @pl.when(p != b)
                 def _():
                     send_copy(p, b).start()
 
+    pl.semaphore_wait(round_sem.at[0], len(row_mates))
+    send([(z + 3) % NZ, (z + NZ - 3) % NZ])
+    pl.semaphore_wait(round_sem.at[2], len(row_mates))
+
+    def far_first(n, carry):
+        k = 6 - n - n // 3
+        back = k - jnp.where(n < 2, 1, jnp.where(n == 2, 2, jnp.where(n == 3, 1, k)))
+        send([(z + k) % NZ, (z + NZ - back) % NZ])
         return carry
 
-    pl.semaphore_wait(round_sem.at[1], len(row_mates))
-    lax.fori_loop(0, NZ // 2, send, 0)
+    lax.fori_loop(0, 5, far_first, 0)
     rc_s[b] = s_s[b]
 
-    for ix in range(3, ROWS, 4):
-        finish_row(ix)
+    for slot in (1, 3, 5, 6, 7):
+        halo_wait(slot)
+    add = edge_lanes(True)
+    for ix in range(ROWS):
+        nt_s[pl.ds(ix, C, stride=ROWS), :] = finish_row(ix, add)
     for n in range(8):
         halo_copy(n).wait_send()
 
@@ -360,7 +371,7 @@
             pltpu.SemaphoreType.DMA((8,)),
             pltpu.SemaphoreType.DMA((8,)), pltpu.SemaphoreType.DMA((8,)),
             pltpu.SemaphoreType.DMA((NB,)), pltpu.SemaphoreType.DMA((NB,)),
-            pltpu.SemaphoreType.REGULAR((2,)),
+            pltpu.SemaphoreType.REGULAR((3,)),
         ],
         compiler_params=pltpu.CompilerParams(
             collective_id=0, has_side_effects=True, vmem_limit_bytes=GRANT - 1536 * 1024

time: 44.3 us -> 42.5 us (0.959)
  Pallas kernels: 43.5 us -> 41.7 us
    pallas_call x1, Pallas kernels: 42.4 us -> 40.6 us  [on_device(): pl.pallas_call(step_kernel, out_shape=moved, in_specs=[hbm] * 8, out_spec...]
where the time goes in v3:
time: 42.5 us; the launch traced here: 42.3 us
  Pallas kernels  41.7 us (98%)
  between operations  0.64 us (2%)
    pallas_call x1, Pallas kernels, on_device(): pl.pallas_call(step_kernel, out_shape=moved, in_specs=[hbm] * 8, out_spec...  40.6 us
    pallas_call x1, Pallas kernels, on_device(): pl.pallas_call(write_kernel, out_shape=(jax.ShapeDtypeStruct((C * ROWS, L...  1.09 us

profile of v3, /device:TPU:1, one launch (start us, length us, event | category | flops | bytes accessed | tf_op | source)
XLA Modules:
  0.0 42.3 jit_solution(1233414948857276046)
XLA Ops:
  0.6 40.6 %transport_condense.1 = (f32[1536,128]{1,0:T(8,128)S(1)}, f32[48,18,128]{2,1,0:T(8,128)S(1)}) custom-call(f32[1536,128]{1,0:T(8,128)} %bitcast.5, f32[1024,128]{1,0:T(8,128)} %bitcast.6, f32[16,128]{1,0:T(8,128)} %m_hbm.1, f32[32,1152]{1,0:T(8,128)} %bitcast.7, s32[1,1152]{1,0:T(1,128)} %o_hbm.1, s32[1,1152]{1,0:T(1,128)} %d_hbm.1, ...), custom_call_target="tpu_custom_call" | custom-call | tf_op jit(solution)/shard_map/transport_condense/pallas_call | solution.py:358
  41.2 1.1 %write_results.1 = (f32[1536,128]{1,0:T(8,128)}, f32[96,1152]{1,0:T(8,128)}) custom-call(f32[1536,128]{1,0:T(8,128)S(1)} %get-tuple-element.6.nt_s, f32[48,18,128]{2,1,0:T(8,128)S(1)} %get-tuple-element.7.rc_s), custom_call_target="tpu_custom_call" | custom-call | tf_op jit(solution)/shard_map/write_results/pallas_call | solution.py:390

commit v4 on v3

--- a/solution.py
+++ b/solution.py
@@ -79,7 +79,7 @@
     r_hbm, v_hbm, m_hbm, t_hbm, o_hbm, d_hbm, k_hbm, e_hbm,
     nt_s, rc_s,
     r_s, v_s, m_s, t_s, o_s, d_s, k_s, e_s,
-    w_s, edge_s, hx_s, he_s, tg_s, dg_s, oh_s, xt_s, s_s,
+    w_s, edge_s, hx_s, he_s, tg_s, dg_s, oh_s, xt_s, s_s, head_s, pack_s, turned_s,
     in_sem, hsend, hrecv, ssem, rsem, round_sem,
 ):
     f, b = lax.axis_index("face"), lax.axis_index("blk")
@@ -194,10 +194,6 @@
                 want == site + 96 * j, F32(1.0), F32(0.0)
             ).astype(BF16)
 
-    pl.semaphore_wait(round_sem.at[1], 2)
-    greet(round_sem.at[2], row_mates)
-    for slot in (0, 2, 4):
-        halo_wait(slot)
 
     pos = lane % 32
 
@@ -225,7 +221,9 @@
                 s = s + hx_s[0, 8 * v : 8 * v + 8, :]
             if ix == ROWS - 1:
                 s = s + hx_s[1, 8 * v : 8 * v + 8, :]
-            far = pltpu.roll(add[rv], (2 * LANES - (2 * ix + 1 + 32 * g)) % LANES, 1)
+            far = F32(0.0)
+            if add is not None:
+                far = pltpu.roll(add[rv], (2 * LANES - (2 * ix + 1 + 32 * g)) % LANES, 1)
             other = jnp.where(
                 lane % 4 == 3,
                 pltpu.roll(s, LANES - 1, 1),
@@ -239,13 +237,13 @@
 
     level = lax.broadcasted_iota(jnp.int32, (LEV, LANES), 0)
 
-    def physics(j, new):
+    def physics(new, warmth, day):
         vapour, heavy, deuter = new[:LEV], new[LEV : 2 * LEV], new[2 * LEV :]
         depth = F32(absorb_coef) * vapour
         for shift in (1, 2, 4, 8, 16):
             depth = depth + jnp.where(level >= shift, pltpu.roll(depth, shift, 0), F32(0.0))
         heating = F32(heat_gain * absorb_coef) * vapour * jnp.exp(-depth)
-        warmed = tg_s[j] + jnp.where(dg_s[j][:1] == 1.0, heating, F32(0.0))
+        warmed = warmth + jnp.where(day == 1.0, heating, F32(0.0))
         saturation = F32(sat_base) * jnp.exp(F32(clausius) * (warmed - F32(ref_temp)))
         remain = jnp.minimum(vapour, saturation)
         log_ratio = jnp.log(remain / vapour)
@@ -253,14 +251,48 @@
         alpha_heavy = jnp.exp(F32(1137.0) * inverse * inverse - F32(0.4156) * inverse - F32(0.0020667))
         alpha_deut = jnp.exp(F32(24844.0) * inverse * inverse - F32(76.248) * inverse + F32(0.052612))
         out = [remain, heavy * jnp.exp(alpha_heavy * log_ratio), deuter * jnp.exp(alpha_deut * log_ratio)]
-        out = jnp.concatenate(out + [jnp.zeros((LEV, LANES), F32)], axis=0).T
-        hi, lo = split(out)
-        xt_s[LANES * j : LANES * (j + 1), :LANES] = hi
-        xt_s[LANES * j : LANES * (j + 1), LANES:] = lo
-
+        return jnp.concatenate(out + [jnp.zeros((LEV, LANES), F32)], axis=0).T
+
+    def put(row, values):
+        hi, lo = split(values)
+        xt_s[row : row + values.shape[0], :LANES] = hi
+        xt_s[row : row + values.shape[0], LANES:] = lo
+
+    wide = lax.broadcasted_iota(jnp.int32, (1, LANES), 1)
+    ratio0 = jnp.full((C, LANES), F32(1.0))
+    warm0 = jnp.full((LEV, LANES), F32(ref_temp))
+    day0 = jnp.zeros((8, LANES), F32)
+    for j, ix in enumerate(KEEP):
+        if ix == 0:
+            continue
+        out = physics(finish_row(ix, None), tg_s[j], dg_s[j][:1])
+        put(LANES * j, out)
+        head_s[j] = out[:16]
+        here = wide == 2 * ix + 1
+        ratio0 = jnp.where(here, pltpu.roll(r_s[pl.ds(ix, C, stride=ROWS), :], 2 * ix + 1, 1), ratio0)
+        warm0 = jnp.where(here, pltpu.roll(tg_s[j], 2 * ix + 1, 1), warm0)
+        day0 = jnp.where(here, pltpu.roll(dg_s[j], 2 * ix + 1, 1), day0)
+    pack_s[:C] = ratio0
+    pack_s[C : C + LEV] = warm0
+    pack_s[C + LEV :] = day0
+
+    pl.semaphore_wait(round_sem.at[1], 2)
+    greet(round_sem.at[2], row_mates)
+    for slot in (0, 2, 4):
+        halo_wait(slot)
     add = edge_lanes(False)
+    put(0, physics(finish_row(0, add), tg_s[0], dg_s[0][:1]))
+    sums = [edge_s[8 * rv : 8 * rv + 8, :] + add[rv] for rv in range(4)]
+    rate = F32(time_step) / jnp.where((wide < 32) & (wide % 2 == 1), sums[3], F32(1.0))
+    lanes0 = [
+        pack_s[8 * v : 8 * v + 8] + rate * pltpu.roll(sums[v % 3], (LANES - 32 * (v // 3)) % LANES, 1)
+        for v in range(C // 8)
+    ]
+    turned_s[...] = physics(jnp.concatenate(lanes0, axis=0), pack_s[C : C + LEV], pack_s[C + LEV : C + LEV + 1])
+    first = lax.broadcasted_iota(jnp.int32, (16, LANES), 0) == 0
     for j, ix in enumerate(KEEP):
-        physics(j, finish_row(ix, add))
+        if ix != 0:
+            put(LANES * j, jnp.where(first, turned_s[2 * ix + 1 : 2 * ix + 2, :], head_s[j]))
 
     row8 = lax.broadcasted_iota(jnp.int32, (1, 8, LANES), 1)
     lane8 = lax.broadcasted_iota(jnp.int32, (1, 8, LANES), 2)
@@ -268,7 +300,7 @@
 
     def send_copy(p, slot):
         return pltpu.make_async_remote_copy(
-            s_s.at[p], rc_s.at[slot], ssem.at[p], rsem.at[slot], device_id=(f, p), device_id_type=MESH
+            s_s.at[p], rc_s.at[slot], ssem.at[0], rsem.at[0], device_id=(f, p), device_id_type=MESH
         )
 
     def send(rows_of_z):
@@ -314,15 +346,10 @@
     for n in range(8):
         halo_copy(n).wait_send()
 
-    def arrive(i, carry):
-        @pl.when(i != b)
-        def _():
-            send_copy(i, b).wait_send()
-            send_copy(i, i).wait_recv()
-
-        return carry
-
-    lax.fori_loop(0, NB, arrive, 0)
+    others = pl.ds(0, NB - 1)
+    pltpu.make_async_remote_copy(
+        s_s.at[others], rc_s.at[others], ssem.at[0], rsem.at[0], device_id=(f, bn), device_id_type=MESH
+    ).wait()
 
 
 def write_kernel(nt_s, rc_s, nt_hbm, ph_hbm, ph_s, sem):
@@ -368,9 +395,10 @@
             vm(12, LEV, LANES), vm(12, 8, LANES),
             vm(SITES, 12 * LANES, dtype=BF16), vm(12 * LANES, 2 * LANES, dtype=BF16),
             vm(NB, MSG, LANES),
+            vm(12, 16, LANES), vm(C + LEV + 8, LANES), vm(LANES, LANES),
             pltpu.SemaphoreType.DMA((8,)),
             pltpu.SemaphoreType.DMA((8,)), pltpu.SemaphoreType.DMA((8,)),
-            pltpu.SemaphoreType.DMA((NB,)), pltpu.SemaphoreType.DMA((NB,)),
+            pltpu.SemaphoreType.DMA((1,)), pltpu.SemaphoreType.DMA((1,)),
             pltpu.SemaphoreType.REGULAR((3,)),
         ],
         compiler_params=pltpu.CompilerParams(

time: 42.5 us -> 41.2 us (0.969)
  Pallas kernels: 41.7 us -> 40.4 us
    pallas_call x1, Pallas kernels: 40.6 us -> 39.3 us  [on_device(): pl.pallas_call(step_kernel, out_shape=moved, in_specs=[hbm] * 8, out_spec...]
where the time goes in v4:
time: 41.2 us; the launch traced here: 41 us
  Pallas kernels  40.4 us (98%)
  between operations  0.64 us (2%)
    pallas_call x1, Pallas kernels, on_device(): pl.pallas_call(step_kernel, out_shape=moved, in_specs=[hbm] * 8, out_spec...  39.3 us
    pallas_call x1, Pallas kernels, on_device(): pl.pallas_call(write_kernel, out_shape=(jax.ShapeDtypeStruct((C * ROWS, L...  1.09 us

profile of v4, /device:TPU:1, one launch (start us, length us, event | category | flops | bytes accessed | tf_op | source)
XLA Modules:
  0.0 41.0 jit_solution(17367422935346335596)
XLA Ops:
  0.6 39.3 %transport_condense.1 = (f32[1536,128]{1,0:T(8,128)S(1)}, f32[48,18,128]{2,1,0:T(8,128)S(1)}) custom-call(f32[1536,128]{1,0:T(8,128)} %bitcast.5, f32[1024,128]{1,0:T(8,128)} %bitcast.6, f32[16,128]{1,0:T(8,128)} %m_hbm.1, f32[32,1152]{1,0:T(8,128)} %bitcast.7, s32[1,1152]{1,0:T(1,128)} %o_hbm.1, s32[1,1152]{1,0:T(1,128)} %d_hbm.1, ...), custom_call_target="tpu_custom_call" | custom-call | tf_op jit(solution)/shard_map/transport_condense/pallas_call | solution.py:385
  39.9 1.1 %write_results.1 = (f32[1536,128]{1,0:T(8,128)}, f32[96,1152]{1,0:T(8,128)}) custom-call(f32[1536,128]{1,0:T(8,128)S(1)} %get-tuple-element.6.nt_s, f32[48,18,128]{2,1,0:T(8,128)S(1)} %get-tuple-element.7.rc_s), custom_call_target="tpu_custom_call" | custom-call | tf_op jit(solution)/shard_map/write_results/pallas_call | solution.py:418

commit v5 on v4

--- a/solution.py
+++ b/solution.py
@@ -151,8 +151,7 @@
         edge_s[8 * rv : 8 * rv + 8, :] = edge[rv]
 
     pl.semaphore_wait(barrier, len(near))
-    greet(round_sem.at[1], column_mates[4:])
-    greet(round_sem.at[0], row_mates)
+    greet(round_sem.at[0], column_mates[4:])
 
     def halo_copy(n):
         src = w_s.at[0] if n == 0 else w_s.at[ROWS - 1] if n == 1 else edge_s
@@ -276,8 +275,8 @@
     pack_s[C : C + LEV] = warm0
     pack_s[C + LEV :] = day0
 
-    pl.semaphore_wait(round_sem.at[1], 2)
-    greet(round_sem.at[2], row_mates)
+    pl.semaphore_wait(round_sem.at[0], 2)
+    greet(round_sem.at[1], row_mates)
     for slot in (0, 2, 4):
         halo_wait(slot)
     add = edge_lanes(False)
@@ -325,17 +324,13 @@
                 def _():
                     send_copy(p, b).start()
 
-    pl.semaphore_wait(round_sem.at[0], len(row_mates))
-    send([(z + 3) % NZ, (z + NZ - 3) % NZ])
-    pl.semaphore_wait(round_sem.at[2], len(row_mates))
+    pl.semaphore_wait(round_sem.at[1], len(row_mates))
 
     def far_first(n, carry):
-        k = 6 - n - n // 3
-        back = k - jnp.where(n < 2, 1, jnp.where(n == 2, 2, jnp.where(n == 3, 1, k)))
-        send([(z + k) % NZ, (z + NZ - back) % NZ])
+        send([(z + 6 - n) % NZ, (z + NZ - 5 + n) % NZ])
         return carry
 
-    lax.fori_loop(0, 5, far_first, 0)
+    lax.fori_loop(0, 6, far_first, 0)
     rc_s[b] = s_s[b]
 
     for slot in (1, 3, 5, 6, 7):
@@ -399,7 +394,7 @@
             pltpu.SemaphoreType.DMA((8,)),
             pltpu.SemaphoreType.DMA((8,)), pltpu.SemaphoreType.DMA((8,)),
             pltpu.SemaphoreType.DMA((1,)), pltpu.SemaphoreType.DMA((1,)),
-            pltpu.SemaphoreType.REGULAR((3,)),
+            pltpu.SemaphoreType.REGULAR((2,)),
         ],
         compiler_params=pltpu.CompilerParams(
             collective_id=0, has_side_effects=True, vmem_limit_bytes=GRANT - 1536 * 1024

time: 41.2 us -> 41.1 us (level)
  no operation moved by 1% of the time
where the time goes in v5:
time: 41.1 us; the launch traced here: 41 us
  Pallas kernels  40.3 us (98%)
  between operations  0.64 us (2%)
    pallas_call x1, Pallas kernels, on_device(): pl.pallas_call(step_kernel, out_shape=moved, in_specs=[hbm] * 8, out_spec...  39.2 us
    pallas_call x1, Pallas kernels, on_device(): pl.pallas_call(write_kernel, out_shape=(jax.ShapeDtypeStruct((C * ROWS, L...  1.09 us

profile of v5, /device:TPU:1, one launch (start us, length us, event | category | flops | bytes accessed | tf_op | source)
XLA Modules:
  0.0 41.0 jit_solution(4789807687379232171)
XLA Ops:
  0.6 39.2 %transport_condense.1 = (f32[1536,128]{1,0:T(8,128)S(1)}, f32[48,18,128]{2,1,0:T(8,128)S(1)}) custom-call(f32[1536,128]{1,0:T(8,128)} %bitcast.5, f32[1024,128]{1,0:T(8,128)} %bitcast.6, f32[16,128]{1,0:T(8,128)} %m_hbm.1, f32[32,1152]{1,0:T(8,128)} %bitcast.7, s32[1,1152]{1,0:T(1,128)} %o_hbm.1, s32[1,1152]{1,0:T(1,128)} %d_hbm.1, ...), custom_call_target="tpu_custom_call" | custom-call | tf_op jit(solution)/shard_map/transport_condense/pallas_call | solution.py:380
  39.9 1.1 %write_results.1 = (f32[1536,128]{1,0:T(8,128)}, f32[96,1152]{1,0:T(8,128)}) custom-call(f32[1536,128]{1,0:T(8,128)S(1)} %get-tuple-element.6.nt_s, f32[48,18,128]{2,1,0:T(8,128)S(1)} %get-tuple-element.7.rc_s), custom_call_target="tpu_custom_call" | custom-call | tf_op jit(solution)/shard_map/write_results/pallas_call | solution.py:413
